TPU v7x, 128 devices: a whole 4x4x4 slice. The times are simulated.
128 devices in a mesh: row: 8 (over z, core), col: 16 (over y, x).
Axes of the slice: x: 4, y: 4, z: 4, core: 2. Of those that a mesh axis runs over, the one named last changes fastest.
Arguments:
- panel_block: float32 [512, 512], P(('row', 'col')), may hold values from -1 to 10, as said below
- panel_cross: float32 [8192, 512], P('col'), may hold values from -0.375 to 0.375
- trail_block: float32 [8192, 8192], P('row', 'col'), may hold values from -1.2 to 1.2
- panel_pixels: float32 [512, 32768], P('row', 'col'), may hold values from -0.375 to 0.375
- trail_pixels: float32 [8192, 32768], P('row', 'col'), may hold values from -1.2 to 1.2
- panel_sectors: float32 [512, 1024], P('row'), may hold values from -6 to 6
- trail_sectors: float32 [8192, 1024], P('col', 'row'), may hold values from -1.2 to 1.2
Outputs:
- panel_factor: float32 [512, 512], P(('row', 'col'))
- panel_columns: float32 [8192, 512], P('col')
- trail_updated: float32 [8192, 8192], P('row', 'col')
- pixels_updated: float32 [8192, 32768], P('row', 'col')
- sectors_updated: float32 [8192, 1024], P('col', 'row')
- prediction: float32 [32768, 1024], P('col', 'row')
Inputs may be any that keep to these rules, and one draw needn't show every extreme that they name: `panel_block`: symmetric positive definite.
All inputs are finite; a program needn't handle non-finite values.
Results may differ from a plain program's by a relative error of at most 0.000075.
Values sent between devices are 32-bit elements; how exact they have to be, the bound alone decides.
A program may use at most 128 MiB of HBM per device.

v0:
```python
import functools

import jax
import jax.numpy as jnp
from jax import lax
from jax.experimental import pallas as pl
from jax.experimental.pallas import tpu as pltpu
from jax.sharding import PartitionSpec as P

HIGHEST = lax.Precision.HIGHEST
MESH = pl.DeviceIdType.MESH
TILE = (8, 128)
CHUNKS = 4


def dot_nn(a, b):
    return lax.dot_general(
        a, b, (((1,), (0,)), ((), ())), precision=HIGHEST, preferred_element_type=jnp.float32
    )


def dot_nt(a, b):
    return lax.dot_general(
        a, b, (((1,), (1,)), ((), ())), precision=HIGHEST, preferred_element_type=jnp.float32
    )


def invert_tile(block, store, after):
    lane = lax.broadcasted_iota(jnp.int32, TILE, 1)
    sub = lax.broadcasted_iota(jnp.int32, TILE, 0)
    here = [sub == j for j in range(8)]
    zero = jnp.zeros(TILE, jnp.float32)
    lane_all = lax.broadcasted_iota(jnp.int32, (128, 128), 1)

    for g in range(16):
        first = 8 * g
        top = block[:8]
        in_group = (lane >= first) & (lane < first + 8)
        unit = (lane - first == sub).astype(jnp.float32)
        pivot = [jnp.broadcast_to(top[:, first + k : first + k + 1], TILE) for k in range(8)]
        rest = lax.select(in_group, unit, top)
        inverse = zero
        for j in range(8):
            row = jnp.broadcast_to(rest[j : j + 1], TILE)
            entry = {k: jnp.broadcast_to(pivot[k][j : j + 1], TILE) for k in range(j, 8)}
            recip = 1.0 / entry[j]
            inverse = lax.select(here[j], row * lax.rsqrt(entry[j]), inverse)
            factor = lax.select(here[j], -recip, pivot[j] * recip)
            rest = lax.select(here[j], zero, rest) - factor * row
            for k in range(j + 1, 8):
                pivot[k] = lax.select(here[j], zero, pivot[k]) - factor * entry[k]
        store(g, lax.select(lane < first + 8, inverse, zero))
        if g < 15:
            below = block[8:]
            shape = below.shape
            lane_b = lane_all[: shape[0]]
            value = lax.select(
                (lane_b >= first) & (lane_b < first + 8), jnp.zeros(shape, jnp.float32), below
            )
            for k in range(8):
                value = value - jnp.broadcast_to(
                    below[:, first + k : first + k + 1], shape
                ) * jnp.broadcast_to(rest[k : k + 1], shape)
            block = value
        after(g)


def panel_kernel(
    own_ref, cross_ref, pixel_ref, sector_ref,
    inverse_ref, rows_ref, pixels_ref, sectors_ref,
    all_ref, m_ref, block_send, block_recv, cross_send, cross_recv, pixel_send, pixel_recv,
    sector_send, sector_recv, local_sem,
):
    row, col = lax.axis_index("row"), lax.axis_index("col")
    z, core = row // 2, lax.rem(row, 2)
    y, x = col // 4, lax.rem(col, 4)

    def turn(value, k):
        return lax.rem(value + k, 4)

    twin = (z * 2 + 1 - core, col)
    plane = [(row, turn(y, k // 4) * 4 + turn(x, k % 4)) for k in range(1, 16)]
    z_peer = [None] + [(turn(z, k) * 2 + core, col) for k in (1, 2, 3)]
    other_z = [None] + [(turn(z, k) * 2 + 1 - core, col) for k in (1, 2, 3)]
    x_peer = [None] + [(row, y * 4 + turn(x, k)) for k in (1, 2, 3)]
    y_peer = [None] + [(row, turn(y, k) * 4 + x) for k in (1, 2, 3)]

    barrier = pltpu.get_barrier_semaphore()
    partners = plane + z_peer[1:] + other_z[1:] + [twin]
    for peer in partners:
        pl.semaphore_signal(barrier, inc=1, device_id=peer, device_id_type=MESH)
    me = row * 16 + col
    all_ref[pl.ds(me, 1)] = own_ref[...]
    pl.semaphore_wait(barrier, len(partners))

    sent = []

    def send(src, dst, send_sem, recv_sem, peer, keep=True):
        copy = pltpu.make_async_remote_copy(
            src_ref=src, dst_ref=dst, send_sem=send_sem, recv_sem=recv_sem,
            device_id=peer, device_id_type=MESH,
        )
        copy.start()
        if keep:
            sent.append(copy)
        return copy

    def arrive(ref, sem):
        pltpu.make_async_copy(ref, ref, sem).wait()

    for k in range(1, 16):
        part = all_ref.at[pl.ds(me, 1)]
        send(part, part, block_send.at[k - 1], block_recv.at[k - 1], plane[k - 1])

    half = 256
    step = half // CHUNKS

    def slot(which, holder):
        same = 1 - jnp.abs(which // 2 - holder)
        odd = lax.rem(which, 2)
        return same * (2 * odd + holder) + (1 - same) * (4 + odd)

    holds = y == z
    my_slot = slot(x, core)

    def cross_part(q):
        return cross_ref.at[pl.ds(core * half + q * step, step)]

    def rows_part(s, q):
        return rows_ref.at[s, pl.ds(q * step, step)]

    def y_copy(q, k):
        return pltpu.make_async_remote_copy(
            src_ref=cross_part(q), dst_ref=rows_part(my_slot, q),
            send_sem=cross_send.at[0, q, k - 1], recv_sem=cross_recv.at[0, q],
            device_id=y_peer[k], device_id_type=MESH,
        )

    def own_copy(q):
        return pltpu.make_async_copy(cross_part(q), rows_part(my_slot, q), cross_recv.at[0, q])

    @pl.when(holds)
    def _():
        for q in range(CHUNKS):
            own_copy(q).start()
        for q in range(CHUNKS):
            for k in (1, 3, 2):
                y_copy(q, k).start()

    def pass_x(q):
        arrive(rows_part(my_slot, q), cross_recv.at[0, q])
        for i, k in enumerate((1, 3)):
            send(rows_part(my_slot, q), rows_part(my_slot, q),
                 cross_send.at[1, q, i], cross_recv.at[1 + i, q], x_peer[k])

    def pass_on(q):
        for i, k in enumerate((1, 3)):
            s = slot(turn(x, 4 - k), core)
            arrive(rows_part(s, q), cross_recv.at[1 + i, q])
            piece = rows_ref.at[s, pl.ds(q * step + i * (step // 2), step // 2)]
            send(piece, piece, cross_send.at[2, q, i], cross_recv.at[3 + i, q], x_peer[k])

    def far_x(q):
        s = slot(turn(x, 2), core)
        for i in range(2):
            piece = rows_ref.at[s, pl.ds(q * step + i * (step // 2), step // 2)]
            arrive(piece, cross_recv.at[3 + i, q])

    def twin_rows(part, parts):
        size = half // parts
        for j in range(2):
            send(rows_ref.at[4 + j, pl.ds(part * size, size)],
                 rows_ref.at[2 * j + core, pl.ds(part * size, size)],
                 cross_send.at[3, part, j], cross_recv.at[5 + j, part], twin)

    def twin_rows_arrive(part, parts):
        size = half // parts
        for j in range(2):
            arrive(rows_ref.at[2 * j + 1 - core, pl.ds(part * size, size)],
                   cross_recv.at[5 + j, part])

    def pixel_rows(owner_row, start, count):
        return pixels_ref.at[pl.ds(owner_row * 64 + start, count)]

    def pixels_start():
        local = pltpu.make_async_copy(pixel_ref, pixel_rows(row, 0, 64), local_sem.at[0])
        local.start()
        for q in range(2):
            for i, k in enumerate((1, 3)):
                send(pixel_ref.at[pl.ds(32 * q, 32)], pixel_rows(row, 32 * q, 32),
                     pixel_send.at[0, q, i], pixel_recv.at[0, q, i], z_peer[k])
        send(pixel_ref, pixel_rows(row, 0, 64), pixel_send.at[2, 0, 0], pixel_recv.at[2, 0, 0], twin)
        return local

    def pixels_on(q):
        for i, k in enumerate((1, 3)):
            owner = turn(z, 4 - k) * 2 + core
            arrive(pixel_rows(owner, 32 * q, 32), pixel_recv.at[0, q, i])
            piece = pixel_rows(owner, 32 * q + 16 * i, 16)
            send(piece, piece, pixel_send.at[1, q, i], pixel_recv.at[1, q, i], z_peer[k])
            whole = pixel_rows(owner, 32 * q, 32)
            send(whole, whole, pixel_send.at[3, q, i], pixel_recv.at[3, q, i], twin)

    def pixels_far(q):
        owner = turn(z, 2) * 2 + core
        for i in range(2):
            piece = pixel_rows(owner, 32 * q + 16 * i, 16)
            arrive(piece, pixel_recv.at[1, q, i])
        whole = pixel_rows(owner, 32 * q, 32)
        send(whole, whole, pixel_send.at[4, q, 0], pixel_recv.at[4, q, 0], twin)

    def pixels_end():
        arrive(pixel_rows(z * 2 + 1 - core, 0, 64), pixel_recv.at[2, 0, 0])
        for q in range(2):
            for i, k in enumerate((1, 3)):
                arrive(pixel_rows(turn(z, 4 - k) * 2 + 1 - core, 32 * q, 32), pixel_recv.at[3, q, i])
            arrive(pixel_rows(turn(z, 2) * 2 + 1 - core, 32 * q, 32), pixel_recv.at[4, q, 0])

    def sector_columns(owner_row):
        return sector_ref.at[:, pl.ds(pl.multiple_of(owner_row * 128, 128), 128)]

    sector_peers = z_peer[1:] + other_z[1:] + [twin]
    peer_rows = [p[0] for p in sector_peers]

    def sectors_start():
        mine = sectors_ref.at[pl.ds(row * 64, 64)]
        local = pltpu.make_async_copy(sector_columns(row), mine, local_sem.at[1])
        local.start()
        for i, peer in enumerate(sector_peers):
            send(sector_columns(peer_rows[i]), mine, sector_send.at[i], sector_recv.at[i], peer)
        return local

    def sectors_end():
        for i in range(7):
            if i == 6:
                source = z * 2 + 1 - core
            else:
                other = (i // 3)
                back = turn(z, 4 - (i % 3 + 1))
                source = back * 2 + (core if other == 0 else 1 - core)
            arrive(sectors_ref.at[pl.ds(source * 64, 64)], sector_recv.at[i])

    for k in range(1, 16):
        source = row * 16 + turn(y, (16 - k) // 4 if k % 4 == 0 else 4 - k // 4) * 4 + turn(x, 4 - k % 4)
        arrive(all_ref.at[pl.ds(source, 1)], block_recv.at[k - 1])

    def block_part(zs, which):
        return all_ref.at[pl.ds(zs * 32 + which * 16, 16), :, pl.ds(0, 128 * (zs + 1))]

    def block_copies(zs):
        part = block_part(zs, core)
        return [
            pltpu.make_async_remote_copy(
                src_ref=part, dst_ref=part, send_sem=block_send.at[14 + k],
                recv_sem=block_recv.at[15 + zs], device_id=z_peer[k], device_id_type=MESH,
            )
            for k in (1, 2, 3)
        ]

    def block_twin(zs):
        part = block_part(zs, core)
        return pltpu.make_async_remote_copy(
            src_ref=part, dst_ref=part, send_sem=block_send.at[18 + zs],
            recv_sem=block_recv.at[19 + zs], device_id=twin, device_id_type=MESH,
        )

    for zs in range(4):
        @pl.when(z == zs)
        def _(zs=zs):
            for copy in block_copies(zs):
                copy.start()
            block_twin(zs).start()

    def block_relay(zs):
        @pl.when(z != zs)
        def _():
            arrive(block_part(zs, core), block_recv.at[15 + zs])
            block_twin(zs).start()

    def block_ready(zs):
        arrive(block_part(zs, 1 - core), block_recv.at[19 + zs])

    def load_rows(zs):
        width = 128 * (zs + 1)
        for i in range(32):
            m_ref[128 * zs + 4 * i : 128 * zs + 4 * i + 4, :width] = all_ref[32 * zs + i, :, :width]

    for q in range(CHUNKS):
        @pl.when(holds)
        def _(q=q):
            arrive(rows_part(my_slot, q), cross_recv.at[0, q])
            for i, k in enumerate((1, 3)):
                pltpu.make_async_remote_copy(
                    src_ref=rows_part(my_slot, q), dst_ref=rows_part(my_slot, q),
                    send_sem=cross_send.at[1, q, i], recv_sem=cross_recv.at[1 + i, q],
                    device_id=x_peer[k], device_id_type=MESH,
                ).start()

    def pass_x_other(q):
        @pl.when(jnp.logical_not(holds))
        def _():
            arrive(rows_part(my_slot, q), cross_recv.at[0, q])
            for i, k in enumerate((1, 3)):
                pltpu.make_async_remote_copy(
                    src_ref=rows_part(my_slot, q), dst_ref=rows_part(my_slot, q),
                    send_sem=cross_send.at[1, q, i], recv_sem=cross_recv.at[1 + i, q],
                    device_id=x_peer[k], device_id_type=MESH,
                ).start()

    block_relay(0)
    local = [pixels_start(), sectors_start()]
    block_ready(0)
    load_rows(0)

    def rest_of_block():
        for zs in (1, 2, 3):
            block_relay(zs)

    plan = {
        (0, 11): [rest_of_block, lambda: pass_x_other(0)],
        (0, 15): [lambda: [(block_ready(zs), load_rows(zs)) for zs in (1, 2, 3)]],
        (1, 3): [lambda: pass_x_other(1), lambda: pass_on(0), lambda: pixels_on(0)],
        (1, 11): [lambda: pass_x_other(2), lambda: pass_on(1)],
        (2, 3): [lambda: pass_x_other(3), lambda: pass_on(2), lambda: pixels_on(1), lambda: pixels_far(0)],
        (2, 11): [lambda: far_x(0), lambda: far_x(1), lambda: twin_rows(0, 2)],
        (3, 0): [lambda: pass_on(3)],
        (3, 7): [lambda: pixels_far(1)],
        (3, 15): [lambda: far_x(2), lambda: far_x(3), lambda: twin_rows(1, 2)],
    }

    n = inverse_ref.shape[0]
    inverse_ref[...] = jnp.zeros_like(inverse_ref)
    for b in range(n // 128):
        s, e = b * 128, b * 128 + 128

        def store(g, value):
            inverse_ref[s + 8 * g : s + 8 * g + 8, s:e] = value

        def after(g):
            for action in plan.get((b, g), ()):
                action()

        invert_tile(m_ref[s:e, s:e], store, after)
        inverse = inverse_ref[s:e, s:e]
        if b:
            inverse_ref[s:e, :s] = dot_nn(inverse, m_ref[s:e, :s])
        if e < n:
            below = dot_nt(m_ref[e:, s:e], inverse)
            m_ref[e:, e:] -= dot_nt(below, below)
            if b:
                m_ref[e:, :s] -= dot_nn(below, inverse_ref[s:e, :s])
            m_ref[e:, s:e] = -dot_nn(below, inverse)

    pixels_end()
    sectors_end()
    for part in range(2):
        twin_rows_arrive(part, 2)
    for copy in local:
        copy.wait()
    for copy in sent:
        copy.wait_send()

    @pl.when(holds)
    def _():
        for q in range(CHUNKS):
            for k in (1, 2, 3):
                y_copy(q, k).wait_send()

    for q in range(CHUNKS):
        for i, k in enumerate((1, 3)):
            part = rows_part(my_slot, q)
            pltpu.make_async_copy(part, part, cross_send.at[1, q, i]).wait()
    for zs in range(4):
        @pl.when(z == zs)
        def _(zs=zs):
            for copy in block_copies(zs):
                copy.wait_send()
        block_twin(zs).wait_send()


def panel(own, cross, pixels, sectors):
    dma = pltpu.SemaphoreType.DMA
    anywhere = pl.BlockSpec(memory_space=pltpu.HBM)
    return pl.pallas_call(
        panel_kernel,
        out_shape=(
            jax.ShapeDtypeStruct((512, 512), jnp.float32),
            jax.ShapeDtypeStruct((6, 256, 512), jnp.float32),
            jax.ShapeDtypeStruct((512, 2048), jnp.float32),
            jax.ShapeDtypeStruct((512, 128), jnp.float32),
        ),
        in_specs=[pl.BlockSpec(memory_space=pltpu.VMEM), anywhere, anywhere, anywhere],
        out_specs=(pl.BlockSpec(memory_space=pltpu.VMEM), anywhere, anywhere, anywhere),
        scratch_shapes=[
            pltpu.VMEM((128, 4, 512), jnp.float32),
            pltpu.VMEM((512, 512), jnp.float32),
            dma((22,)), dma((23,)),
            dma((4, CHUNKS, 3)), dma((7, CHUNKS)),
            dma((5, 2, 2)), dma((5, 2, 2)),
            dma((7,)), dma((7,)),
            dma((2,)),
        ],
        compiler_params=pltpu.CompilerParams(
            collective_id=0, has_side_effects=True, vmem_limit_bytes=32 << 20
        ),
        name="panel",
    )(own.reshape(1, 4, 512), cross, pixels, sectors)


def shards(
    panel_block, panel_cross, trail_block, panel_pixels, trail_pixels, panel_sectors, trail_sectors
):
    row_index = lax.axis_index("row")
    col_index = lax.axis_index("col")
    inverse, rows, pixels, sectors = panel(panel_block, panel_cross, panel_pixels, panel_sectors)
    cross_rows = rows[:4].reshape(1024, 512)

    def dot(a, b, ca, cb):
        return lax.dot_general(a, b, (((ca,), (cb,)), ((), ())), precision=lax.Precision.HIGH)

    n = inverse.shape[0]
    device_index = row_index * lax.axis_size("col") + col_index
    factor_rows = lax.dot_general(
        panel_block, inverse, (((1,), (1,)), ((), ())), precision=HIGHEST
    )
    own_row = device_index * 4 + lax.broadcasted_iota(jnp.int32, (4, n), 0)
    factor_rows = jnp.where(lax.broadcasted_iota(jnp.int32, (4, n), 1) <= own_row, factor_rows, 0.0)
    column_own = dot(panel_cross, inverse, 1, 1)
    row_block = dot(cross_rows, inverse, 1, 1)
    trail_updated = trail_block - dot(row_block, column_own, 1, 1)
    coupling = dot(row_block, inverse, 1, 0)
    pixel_total = trail_pixels - dot(coupling, pixels, 1, 0)
    solved = dot(inverse, sectors, 1, 0)
    kriging_weights = dot(inverse, solved, 0, 0)
    sectors_updated = trail_sectors - dot(column_own, solved, 1, 0)
    predicted = dot(pixels, kriging_weights, 0, 0)
    return (factor_rows, column_own, trail_updated, pixel_total, sectors_updated, predicted)


def solution(mesh):
    return jax.shard_map(
        shards,
        mesh=mesh,
        in_specs=(
            P(("row", "col"), None),
            P("col", None),
            P("row", "col"),
            P("row", "col"),
            P("row", "col"),
            P("row", None),
            P("col", "row"),
        ),
        out_specs=(
            P(("row", "col"), None),
            P("col", None),
            P("row", "col"),
            P("row", "col"),
            P("col", "row"),
            P("col", "row"),
        ),
        check_vma=False,
    )
```

profile of v0, /device:TPU:1, one launch (start us, length us, event | category | flops | bytes accessed | tf_op | source)
XLA Modules:
  0.0 81.2 jit_solution(9998429071077406628)
XLA Ops:
  0.6 0.0 copy-start
  0.6 1.2 %copy-done = f32[512,512]{1,0:T(8,128)S(1)} copy-done((f32[512,512]{1,0:T(8,128)S(1)}, f32[512,512]{1,0:T(8,128)}, u32[]{:S(2)}) %copy-start) | copy-done | bytes 1048600
  1.9 0.0 copy-start.2
  1.9 1.0 %copy-done.2 = f32[64,2048]{1,0:T(8,128)S(1)} copy-done((f32[64,2048]{1,0:T(8,128)S(1)}, f32[64,2048]{1,0:T(8,128)}, u32[]{:S(2)}) %copy-start.2) | copy-done | bytes 524312
  2.9 0.0 copy-start.3
  2.9 0.9 %copy-done.3 = f32[64,1024]{1,0:T(8,128)S(1)} copy-done((f32[64,1024]{1,0:T(8,128)S(1)}, f32[64,1024]{1,0:T(8,128)}, u32[]{:S(2)}) %copy-start.3) | copy-done | bytes 262168
  3.9 0.0 copy-start.4
  3.9 0.7 copy-done.4
  4.5 47.9 %panel.1 = (f32[512,512]{1,0:T(8,128)S(1)}, f32[6,256,512]{2,1,0:T(8,128)S(1)}, f32[512,2048]{1,0:T(8,128)S(1)}, f32[512,128]{1,0:T(8,128)S(1)}) custom-call(f32[1,4,512]{2,1,0:T(4,128)S(1)} %bitcast.27, f32[512,512]{1,0:T(8,128)S(1)} %copy-done, f32[64,2048]{1,0:T(8,128)S(1)} %copy-done.2, f32[64,1024]{1,0:T(8,128)S(1)} %copy-done.3), custom_call_target="tpu_custom_call" | custom-call | tf_op jit(solution)/shard_map/panel/pallas_call | solution.py:384
  52.5 0.6 fusion.4
  53.1 1.0 %fusion.5 = f32[512,128]{1,0:T(8,128)S(1)} fusion(f32[512,512]{1,0:T(8,128)S(1)} %get-tuple-element.10, f32[512,128]{1,0:T(8,128)S(1)} %fusion.4), kind=kOutput, calls=%fused_computation.11 | convolution fusion | flops 201326592 | bytes 1572864 | tf_op jit(solution)/shard_map/dot_general | solution.py:419
  54.1 0.0 slice-start
  54.1 4.5 %fusion.6 = f32[2048,128]{1,0:T(8,128)} fusion(f32[512,2048]{1,0:T(8,128)S(1)} %get-tuple-element.12, f32[512,128]{1,0:T(8,128)S(1)} %fusion.5), kind=kOutput, calls=%fused_computation.12 | convolution fusion | flops 805306368 | bytes 5505024 | tf_op jit(solution)/shard_map/dot_general | solution.py:419
  58.6 0.2 slice.3
  58.8 0.0 slice-start.1
  58.8 1.9 %fusion.2 = f32[1024,512]{1,0:T(8,128)S(1)} fusion(f32[1024,512]{1,0:T(8,128)S(1)} %bitcast.29, f32[512,512]{1,0:T(8,128)S(1)} %get-tuple-element.10), kind=kOutput, calls=%fused_computation.8 | convolution fusion | flops 1610612736 | bytes 5242880 | tf_op jit(solution)/shard_map/dot_general | solution.py:419
  60.7 1.8 %fusion.3 = f32[1024,512]{1,0:T(8,128)S(1)} fusion(f32[1024,512]{1,0:T(8,128)S(1)} %fusion.2, f32[512,512]{1,0:T(8,128)S(1)} %get-tuple-element.10), kind=kOutput, calls=%fused_computation.9 | convolution fusion | flops 1610612736 | bytes 5242880 | tf_op jit(solution)/shard_map/dot_general | solution.py:419
  62.5 0.0 slice-done
  62.5 0.0 slice-done.1
  62.5 0.0 copy-start.1
  62.6 9.7 %convolution_subtract_fusion = f32[1024,2048]{1,0:T(8,128)} fusion(f32[1024,2048]{1,0:T(8,128)S(1)} %bitcast.31, f32[1024,512]{1,0:T(8,128)S(1)} %fusion.3, f32[512,2048]{1,0:T(8,128)S(1)} %get-tuple-element.12), kind=kOutput, calls=%fused_computation | convolution fusion | flops 6444548096 | bytes 23068672 | tf_op jit(solution)/shard_map/dot_general | solution.py:419
  72.3 0.0 copy-done.1
  72.3 0.0 copy-start.7
  72.3 0.0 copy-start.6
  72.3 1.1 %fusion.1 = f32[512,512]{1,0:T(8,128)S(1)} fusion(f32[512,512]{1,0:T(8,128)S(1)} %get-tuple-element.10, f32[512,512]{1,0:T(8,128)S(1)} %copy-done.1), kind=kOutput, calls=%fused_computation.7 | convolution fusion | flops 805306368 | bytes 3145728 | tf_op jit(solution)/shard_map/dot_general | solution.py:419
  73.3 0.0 copy-done.7
  73.4 1.7 %convolution_subtract_fusion.2 = f32[512,128]{1,0:T(8,128)} fusion(f32[512,128]{1,0:T(8,128)S(1)} %copy-done.7, f32[512,512]{1,0:T(8,128)S(1)} %fusion.1, f32[512,128]{1,0:T(8,128)S(1)} %fusion.4), kind=kOutput, calls=%fused_computation.2 | convolution fusion | flops 201392128 | bytes 1835008 | tf_op jit(solution)/shard_map/dot_general | solution.py:419
  75.1 0.0 copy-done.6
  75.1 3.2 %convolution_subtract_fusion.1 = f32[1024,512]{1,0:T(8,128)} fusion(f32[1024,512]{1,0:T(8,128)S(1)} %copy-done.6, f32[1024,512]{1,0:T(8,128)S(1)} %fusion.2, f32[512,512]{1,0:T(8,128)S(1)} %fusion.1), kind=kOutput, calls=%fused_computation.1 | convolution fusion | flops 1611137024 | bytes 7340032 | tf_op jit(solution)/shard_map/dot_general | solution.py:419
  78.3 0.0 copy-start.5
  78.3 1.3 %copy.13 = f32[512,512]{1,0:T(8,128)} copy(f32[512,512]{0,1:T(8,128)S(1)} %bitcast.28) | data formatting | bytes 2097152
  79.6 0.0 copy-done.5
  79.6 1.6 %fusion = f32[4,512]{1,0:T(4,128)} fusion(f32[512,512]{1,0:T(8,128)S(1)} %get-tuple-element.10, f32[4,512]{1,0:T(4,128)S(1)} %copy-done.5, s32[4]{0:T(128)S(1)} %iota_add_fusion), kind=kOutput, calls=%fused_computation.4 | convolution fusion | flops 12587008 | bytes 1064976 | tf_op jit(solution)/shard_map/dot_general | solution.py:423
  (2 shorter events, 0.0 us)
Async XLA Ops:
  0.6 1.2 %copy-start = (f32[512,512]{1,0:T(8,128)S(1)}, f32[512,512]{1,0:T(8,128)}, u32[]{:S(2)}) copy-start(f32[512,512]{1,0:T(8,128)} %cross_ref.1) | copy-start | bytes 3145732
  1.9 1.0 %copy-start.2 = (f32[64,2048]{1,0:T(8,128)S(1)}, f32[64,2048]{1,0:T(8,128)}, u32[]{:S(2)}) copy-start(f32[64,2048]{1,0:T(8,128)} %pixel_ref.1) | copy-start | bytes 1572868
  2.9 0.9 %copy-start.3 = (f32[64,1024]{1,0:T(8,128)S(1)}, f32[64,1024]{1,0:T(8,128)}, u32[]{:S(2)}) copy-start(f32[64,1024]{1,0:T(8,128)} %sector_ref.1) | copy-start | bytes 786436
  3.9 0.7 copy-start.4
  54.1 8.4 %slice-start = ((s8[8388608]{0:T(1024)(128)(4,1)}), s8[4194304]{0:T(1024)(128)(4,1)S(1)}, s32[]{:S(2)}) async-start(s8[8388608]{0:T(1024)(128)(4,1)} %bitcast.30), calls=%async_computation | async-start | bytes 8388608
  58.8 3.7 %slice-start.1 = ((s8[8388608]{0:T(1024)(128)(4,1)}), s8[4194304]{0:T(1024)(128)(4,1)S(1)}, s32[]{:S(2)}) async-start(s8[8388608]{0:T(1024)(128)(4,1)} %bitcast.30), calls=%async_computation.1 | async-start | bytes 8388608
  62.5 9.7 %copy-start.1 = (f32[512,512]{1,0:T(8,128)S(1)}, f32[512,512]{1,0:T(8,128)}, u32[]{:S(2)}) copy-start(f32[512,512]{1,0:T(8,128)} %cross_ref.1) | copy-start | bytes 3145732
  72.3 1.1 %copy-start.7 = (f32[512,128]{1,0:T(8,128)S(1)}, f32[512,128]{1,0:T(8,128)}, u32[]{:S(2)}) copy-start(f32[512,128]{1,0:T(8,128)} %param.13) | copy-start | bytes 786436
  72.3 2.8 %copy-start.6 = (f32[1024,512]{1,0:T(8,128)S(1)}, f32[1024,512]{1,0:T(8,128)}, u32[]{:S(2)}) copy-start(f32[1024,512]{1,0:T(8,128)} %param.9) | copy-start | bytes 6291460
  78.3 1.3 %copy-start.5 = (f32[4,512]{1,0:T(4,128)S(1)}, f32[4,512]{1,0:T(4,128)}, u32[]{:S(2)}) copy-start(f32[4,512]{1,0:T(4,128)} %param.7) | copy-start | bytes 24580
where the time goes:
time: 81.5 us; the launch traced here: 81.2 us
  Pallas kernels  47.9 us (59%)
  matrix products  27.1 us (33%)
  local copies, waits for them, and re-layouts  5.43 us (7%)
    pallas_call x1, Pallas kernels, panel(): pl.pallas_call(panel_kernel, out_shape=(jax.ShapeDtypeStruct((512, 512),...  47.9 us
    dot_general x9, matrix products, dot(): lax.dot_general(a, b, (((ca,), (cb,)), ((), ())), precision=lax.Precision...  25.5 us
    unnamed x21, local copies, waits for them, and re-layouts  5.25 us

commit v1 on v0

--- a/solution.py
+++ b/solution.py
@@ -271,6 +271,8 @@
                 copy.start()
             block_twin(zs).start()
 
+    local = [pixels_start()]
+
     def block_relay(zs):
         @pl.when(z != zs)
         def _():
@@ -308,24 +310,32 @@
                 ).start()
 
     block_relay(0)
-    local = [pixels_start(), sectors_start()]
     block_ready(0)
     load_rows(0)
+    local.append(sectors_start())
+    pass_x_other(0)
 
     def rest_of_block():
         for zs in (1, 2, 3):
             block_relay(zs)
 
     plan = {
-        (0, 11): [rest_of_block, lambda: pass_x_other(0)],
+        (0, 7): [lambda: pass_x_other(1)],
+        (0, 11): [rest_of_block],
         (0, 15): [lambda: [(block_ready(zs), load_rows(zs)) for zs in (1, 2, 3)]],
-        (1, 3): [lambda: pass_x_other(1), lambda: pass_on(0), lambda: pixels_on(0)],
-        (1, 11): [lambda: pass_x_other(2), lambda: pass_on(1)],
-        (2, 3): [lambda: pass_x_other(3), lambda: pass_on(2), lambda: pixels_on(1), lambda: pixels_far(0)],
-        (2, 11): [lambda: far_x(0), lambda: far_x(1), lambda: twin_rows(0, 2)],
-        (3, 0): [lambda: pass_on(3)],
-        (3, 7): [lambda: pixels_far(1)],
-        (3, 15): [lambda: far_x(2), lambda: far_x(3), lambda: twin_rows(1, 2)],
+        (1, 0): [lambda: pass_on(0)],
+        (1, 3): [lambda: pass_x_other(2)],
+        (1, 8): [lambda: pass_on(1)],
+        (1, 10): [lambda: pixels_on(0)],
+        (1, 13): [lambda: pixels_on(1)],
+        (1, 15): [lambda: pass_x_other(3)],
+        (2, 4): [lambda: pass_on(2), lambda: far_x(0)],
+        (2, 10): [lambda: far_x(1), lambda: twin_rows(0, 2)],
+        (2, 15): [lambda: pass_on(3)],
+        (3, 0): [lambda: pixels_far(0)],
+        (3, 4): [lambda: pixels_far(1)],
+        (3, 8): [lambda: far_x(2)],
+        (3, 12): [lambda: far_x(3), lambda: twin_rows(1, 2)],
     }
 
     n = inverse_ref.shape[0]
@@ -380,7 +390,7 @@
 
 def panel(own, cross, pixels, sectors):
     dma = pltpu.SemaphoreType.DMA
-    anywhere = pl.BlockSpec(memory_space=pltpu.HBM)
+    anywhere = pl.BlockSpec(memory_space=pl.ANY)
     return pl.pallas_call(
         panel_kernel,
         out_shape=(
@@ -401,40 +411,123 @@
             dma((2,)),
         ],
         compiler_params=pltpu.CompilerParams(
-            collective_id=0, has_side_effects=True, vmem_limit_bytes=32 << 20
+            collective_id=0, has_side_effects=True, vmem_limit_bytes=16 << 20
+        ),
+        cost_estimate=pl.CostEstimate(
+            flops=40_000_000_000, bytes_accessed=16 << 20, transcendentals=0
         ),
         name="panel",
     )(own.reshape(1, 4, 512), cross, pixels, sectors)
+
+
+def high_low(value):
+    high = value.astype(jnp.bfloat16)
+    return high, (value - high.astype(jnp.float32)).astype(jnp.bfloat16)
+
+
+def left_cat(value, axis=1):
+    high, low = high_low(value)
+    return jnp.concatenate([high, high, low], axis=axis)
+
+
+def right_cat(value, axis):
+    high, low = high_low(value)
+    return jnp.concatenate([high, low, high], axis=axis)
+
+
+def mxu(a, b, ca, cb):
+    return lax.dot_general(a, b, (((ca,), (cb,)), ((), ())), preferred_element_type=jnp.float32)
+
+
+def product_kernel(
+    own_ref, cross_ref, rows_ref, inverse_ref, sectors_ref, trail_sectors_ref,
+    trail_ref, pixels_ref, trail_pixels_ref,
+    factor_out, columns_out, trail_out, pixels_out, sectors_out, predicted_out,
+    rows_cat, columns_cat, coupling_cat, weights_cat,
+):
+    step = pl.program_id(0)
+    device = lax.axis_index("row") * 16 + lax.axis_index("col")
+
+    @pl.when(step == 0)
+    def _():
+        inverse = inverse_ref[...]
+        by_column = right_cat(inverse, 1)
+        by_row = right_cat(inverse, 0)
+        own = mxu(left_cat(own_ref[...]), by_column, 1, 1)
+        lane = lax.broadcasted_iota(jnp.int32, own.shape, 1)
+        line = lax.broadcasted_iota(jnp.int32, own.shape, 0) + device * 4
+        factor_out[...] = jnp.where(lane <= line, own, 0.0)
+        columns = mxu(left_cat(cross_ref[...]), by_column, 1, 1)
+        columns_out[...] = columns
+        columns_cat[...] = right_cat(columns, 1)
+        for i in range(4):
+            part = slice(256 * i, 256 * i + 256)
+            panel_rows = left_cat(mxu(left_cat(rows_ref[i]), by_column, 1, 1))
+            rows_cat[part] = panel_rows
+            coupling_cat[part] = left_cat(mxu(panel_rows, by_row, 1, 0))
+        solved = mxu(left_cat(inverse), right_cat(sectors_ref[...], 0), 1, 0)
+        solved_cat = right_cat(solved, 0)
+        sectors_out[...] = trail_sectors_ref[...] - mxu(left_cat(columns), solved_cat, 1, 0)
+        weights = mxu(left_cat(inverse.T), solved_cat, 1, 0)
+        weights_cat[...] = left_cat(weights.T)
+
+    width = pixels_out.shape[1]
+    part = pl.ds(pl.multiple_of(step * width, width), width)
+    tile = right_cat(pixels_ref[:, part], 0)
+    pixels_out[...] = trail_pixels_ref[:, part] - mxu(coupling_cat[...], tile, 1, 0)
+    predicted_out[...] = mxu(weights_cat[...], tile, 1, 0).T
+    size = trail_out.shape[0]
+    lines = pl.ds(pl.multiple_of(step * size, size), size)
+    trail_out[...] = trail_ref[lines, :] - mxu(rows_cat[lines, :], columns_cat[...], 1, 1)
+
+
+def products(own, cross, rows, inverse, sectors, trail_sectors, trail, pixels, trail_pixels):
+    n, width = pixels.shape
+    steps = 4
+    height = trail.shape[0]
+
+    def fixed(shape):
+        return pl.BlockSpec(shape, lambda i: (0,) * len(shape), pipeline_mode=pl.Buffered(1))
+
+    f32 = lambda *shape: jax.ShapeDtypeStruct(shape, jnp.float32)
+    bf16 = lambda *shape: pltpu.VMEM(shape, jnp.bfloat16)
+    return pl.pallas_call(
+        product_kernel,
+        grid=(steps,),
+        out_shape=(
+            f32(*own.shape), f32(*cross.shape), f32(*trail.shape), f32(*trail_pixels.shape),
+            f32(*trail_sectors.shape), f32(width, sectors.shape[1]),
+        ),
+        in_specs=[pl.BlockSpec(memory_space=pltpu.VMEM)] * 9,
+        out_specs=(
+            fixed(own.shape), fixed(cross.shape),
+            pl.BlockSpec((height // steps, trail.shape[1]), lambda i: (i, 0)),
+            pl.BlockSpec((height, width // steps), lambda i: (0, i)),
+            fixed(trail_sectors.shape),
+            pl.BlockSpec((width // steps, sectors.shape[1]), lambda i: (i, 0)),
+        ),
+        scratch_shapes=[
+            bf16(height, 3 * n), bf16(cross.shape[0], 3 * n), bf16(height, 3 * n),
+            bf16(sectors.shape[1], 3 * n),
+        ],
+        compiler_params=pltpu.CompilerParams(vmem_limit_bytes=26 << 20),
+        cost_estimate=pl.CostEstimate(
+            flops=13_500_000_000, bytes_accessed=32 << 20, transcendentals=0
+        ),
+        name="products",
+    )(own, cross, rows, inverse, sectors, trail_sectors, trail, pixels, trail_pixels)
 
 
 def shards(
     panel_block, panel_cross, trail_block, panel_pixels, trail_pixels, panel_sectors, trail_sectors
 ):
-    row_index = lax.axis_index("row")
-    col_index = lax.axis_index("col")
-    inverse, rows, pixels, sectors = panel(panel_block, panel_cross, panel_pixels, panel_sectors)
-    cross_rows = rows[:4].reshape(1024, 512)
-
-    def dot(a, b, ca, cb):
-        return lax.dot_general(a, b, (((ca,), (cb,)), ((), ())), precision=lax.Precision.HIGH)
-
-    n = inverse.shape[0]
-    device_index = row_index * lax.axis_size("col") + col_index
-    factor_rows = lax.dot_general(
-        panel_block, inverse, (((1,), (1,)), ((), ())), precision=HIGHEST
+    in_hbm = lambda v: pltpu.with_memory_space_constraint(v, pltpu.HBM)
+    inverse, rows, pixels, sectors = panel(
+        panel_block, in_hbm(panel_cross), in_hbm(panel_pixels), in_hbm(panel_sectors)
     )
-    own_row = device_index * 4 + lax.broadcasted_iota(jnp.int32, (4, n), 0)
-    factor_rows = jnp.where(lax.broadcasted_iota(jnp.int32, (4, n), 1) <= own_row, factor_rows, 0.0)
-    column_own = dot(panel_cross, inverse, 1, 1)
-    row_block = dot(cross_rows, inverse, 1, 1)
-    trail_updated = trail_block - dot(row_block, column_own, 1, 1)
-    coupling = dot(row_block, inverse, 1, 0)
-    pixel_total = trail_pixels - dot(coupling, pixels, 1, 0)
-    solved = dot(inverse, sectors, 1, 0)
-    kriging_weights = dot(inverse, solved, 0, 0)
-    sectors_updated = trail_sectors - dot(column_own, solved, 1, 0)
-    predicted = dot(pixels, kriging_weights, 0, 0)
-    return (factor_rows, column_own, trail_updated, pixel_total, sectors_updated, predicted)
+    return products(
+        panel_block, panel_cross, rows, inverse, sectors, trail_sectors, trail_block, pixels, trail_pixels
+    )
 
 
 def solution(mesh):

time: 81.5 us -> 66 us (0.81)
  matrix products: 27.1 us -> 0 us
  Pallas kernels: 47.9 us -> 64.4 us
  local copies, waits for them, and re-layouts: 5.43 us -> 0.71 us
    dot_general x10 -> x0, matrix products: 27.1 us -> none  [the longest x9 25.5 us: dot(): lax.dot_general(a, b, (((ca,), (cb,)), ((), ())), precision=lax.Precision...]
    pallas_call x0 -> x1, Pallas kernels: none -> 18.7 us  [products(): pl.pallas_call(product_kernel, grid=(steps,), out_shape=(f32(*own.shape),...]
    unnamed x21 -> x12, local copies, waits for them, and re-layouts: 5.25 us -> 0.71 us
    pallas_call x1, Pallas kernels: 47.9 us -> 45.7 us  [panel(): pl.pallas_call(panel_kernel, out_shape=(jax.ShapeDtypeStruct((512, 512),...]
where the time goes in v1:
time: 66 us; the launch traced here: 65.8 us
  Pallas kernels  64.4 us (98%)
  local copies, waits for them, and re-layouts  0.71 us (1%)
  between operations  0.7 us (1%)
    pallas_call x1, Pallas kernels, panel(): pl.pallas_call(panel_kernel, out_shape=(jax.ShapeDtypeStruct((512, 512),...  45.7 us
    pallas_call x1, Pallas kernels, products(): pl.pallas_call(product_kernel, grid=(steps,), out_shape=(f32(*own.shape),...  18.7 us

profile of v1, /device:TPU:1, one launch (start us, length us, event | category | flops | bytes accessed | tf_op | source)
XLA Modules:
  0.0 65.8 jit_solution(14970356547410082971)
XLA Ops:
  0.6 0.0 copy-start.4
  0.6 0.7 %copy-done.4 = f32[4,512]{1,0:T(4,128)S(1)} copy-done((f32[4,512]{1,0:T(4,128)S(1)}, f32[4,512]{1,0:T(4,128)}, u32[]{:S(2)}) %copy-start.4) | copy-done | bytes 8216
  1.3 0.0 copy-start
  1.3 0.0 copy-start.1
  1.3 0.0 copy-start.2
  1.3 0.0 copy-start.3
  1.3 0.0 copy-start.5
  1.4 45.7 %panel.1 = (f32[512,512]{1,0:T(8,128)S(1)}, f32[6,256,512]{2,1,0:T(8,128)S(1)}, f32[512,2048]{1,0:T(8,128)S(1)}, f32[512,128]{1,0:T(8,128)S(1)}) custom-call(f32[1,4,512]{2,1,0:T(4,128)S(1)} %bitcast.1, f32[512,512]{1,0:T(8,128)} %cross_ref.3, f32[64,2048]{1,0:T(8,128)} %pixel_ref.1, f32[64,1024]{1,0:T(8,128)} %sector_ref.1), custom_call_target="tpu_custom_call" | custom-call | flops 40000000000 | bytes 16777216 | tf_op jit(solution)/shard_map/panel/pallas_call | solution.py:394
  47.1 0.0 copy-done
  47.1 0.0 copy-done.1
  47.1 0.0 copy-done.2
  47.1 0.0 copy-done.3
  47.1 0.0 copy-done.5
  47.1 18.7 %products.1 = (f32[4,512]{1,0:T(4,128)}, f32[512,512]{1,0:T(8,128)}, f32[1024,512]{1,0:T(8,128)}, f32[1024,2048]{1,0:T(8,128)}, f32[512,128]{1,0:T(8,128)}, /*index=5*/f32[2048,128]{1,0:T(8,128)}) custom-call(f32[4,512]{1,0:T(4,128)S(1)} %copy-done.5, f32[512,512]{1,0:T(8,128)S(1)} %copy-done.2, f32[6,256,512]{2,1,0:T(8,128)S(1)} %get-tuple-element.10.rows_ref, ...), custom_call_target="tpu_custom_call" | custom-call | flops 13500000256 | bytes 33554432 | tf_op jit(solution)/shard_map/products/pallas_call | solution.py:494
Async XLA Ops:
  0.6 0.7 %copy-start.4 = (f32[4,512]{1,0:T(4,128)S(1)}, f32[4,512]{1,0:T(4,128)}, u32[]{:S(2)}) copy-start(f32[4,512]{1,0:T(4,128)} %own_ref.1) | copy-start | bytes 24580
  1.3 45.7 %copy-start = (f32[1024,2048]{1,0:T(8,128)S(1)}, f32[1024,2048]{1,0:T(8,128)}, u32[]{:S(2)}) copy-start(f32[1024,2048]{1,0:T(8,128)} %trail_pixels_ref.1) | copy-start | bytes 25165828
  1.3 45.7 %copy-start.1 = (f32[1024,512]{1,0:T(8,128)S(1)}, f32[1024,512]{1,0:T(8,128)}, u32[]{:S(2)}) copy-start(f32[1024,512]{1,0:T(8,128)} %trail_ref.1) | copy-start | bytes 6291460
  1.3 45.7 %copy-start.2 = (f32[512,512]{1,0:T(8,128)S(1)}, f32[512,512]{1,0:T(8,128)}, u32[]{:S(2)}) copy-start(f32[512,512]{1,0:T(8,128)} %cross_ref.3) | copy-start | bytes 3145732
  1.3 45.8 %copy-start.3 = (f32[512,128]{1,0:T(8,128)S(1)}, f32[512,128]{1,0:T(8,128)}, u32[]{:S(2)}) copy-start(f32[512,128]{1,0:T(8,128)} %trail_sectors_ref.1) | copy-start | bytes 786436
  1.3 45.8 %copy-start.5 = (f32[4,512]{1,0:T(4,128)S(1)}, f32[4,512]{1,0:T(4,128)}, u32[]{:S(2)}) copy-start(f32[4,512]{1,0:T(4,128)} %own_ref.1) | copy-start | bytes 24580

commit v2 on v1

--- a/solution.py
+++ b/solution.py
@@ -38,17 +38,23 @@
         in_group = (lane >= first) & (lane < first + 8)
         unit = (lane - first == sub).astype(jnp.float32)
         pivot = [jnp.broadcast_to(top[:, first + k : first + k + 1], TILE) for k in range(8)]
+        entry = {
+            (j, k): jnp.broadcast_to(pivot[k][j : j + 1], TILE) for k in range(8) for j in range(k + 1)
+        }
         rest = lax.select(in_group, unit, top)
         inverse = zero
         for j in range(8):
+            recip = 1.0 / entry[j, j]
+            scaled = {k: entry[j, k] * recip for k in range(j + 1, 8)}
+            for i in range(j + 1, 8):
+                for k in range(i, 8):
+                    entry[i, k] = entry[i, k] - scaled[i] * entry[j, k]
             row = jnp.broadcast_to(rest[j : j + 1], TILE)
-            entry = {k: jnp.broadcast_to(pivot[k][j : j + 1], TILE) for k in range(j, 8)}
-            recip = 1.0 / entry[j]
-            inverse = lax.select(here[j], row * lax.rsqrt(entry[j]), inverse)
+            inverse = lax.select(here[j], row * lax.rsqrt(entry[j, j]), inverse)
             factor = lax.select(here[j], -recip, pivot[j] * recip)
             rest = lax.select(here[j], zero, rest) - factor * row
             for k in range(j + 1, 8):
-                pivot[k] = lax.select(here[j], zero, pivot[k]) - factor * entry[k]
+                pivot[k] = lax.select(here[j], zero, pivot[k]) - factor * entry[j, k]
         store(g, lax.select(lane < first + 8, inverse, zero))
         if g < 15:
             below = block[8:]
@@ -68,7 +74,7 @@
 def panel_kernel(
     own_ref, cross_ref, pixel_ref, sector_ref,
     inverse_ref, rows_ref, pixels_ref, sectors_ref,
-    all_ref, m_ref, block_send, block_recv, cross_send, cross_recv, pixel_send, pixel_recv,
+    all_ref, m_ref, below_ref, block_send, block_recv, cross_send, cross_recv, pixel_send, pixel_recv,
     sector_send, sector_recv, local_sem,
 ):
     row, col = lax.axis_index("row"), lax.axis_index("col")
@@ -90,7 +96,8 @@
     for peer in partners:
         pl.semaphore_signal(barrier, inc=1, device_id=peer, device_id_type=MESH)
     me = row * 16 + col
-    all_ref[pl.ds(me, 1)] = own_ref[...]
+    own_rows = pltpu.make_async_copy(own_ref, all_ref.at[pl.ds(me, 1)], local_sem.at[2])
+    own_rows.start()
     pl.semaphore_wait(barrier, len(partners))
 
     sent = []
@@ -110,7 +117,7 @@
 
     for k in range(1, 16):
         part = all_ref.at[pl.ds(me, 1)]
-        send(part, part, block_send.at[k - 1], block_recv.at[k - 1], plane[k - 1])
+        send(own_ref, part, block_send.at[k - 1], block_recv.at[k - 1], plane[k - 1])
 
     half = 256
     step = half // CHUNKS
@@ -185,9 +192,9 @@
     def pixels_start():
         local = pltpu.make_async_copy(pixel_ref, pixel_rows(row, 0, 64), local_sem.at[0])
         local.start()
-        for q in range(2):
+        for q in range(1):
             for i, k in enumerate((1, 3)):
-                send(pixel_ref.at[pl.ds(32 * q, 32)], pixel_rows(row, 32 * q, 32),
+                send(pixel_ref, pixel_rows(row, 0, 64),
                      pixel_send.at[0, q, i], pixel_recv.at[0, q, i], z_peer[k])
         send(pixel_ref, pixel_rows(row, 0, 64), pixel_send.at[2, 0, 0], pixel_recv.at[2, 0, 0], twin)
         return local
@@ -195,26 +202,26 @@
     def pixels_on(q):
         for i, k in enumerate((1, 3)):
             owner = turn(z, 4 - k) * 2 + core
-            arrive(pixel_rows(owner, 32 * q, 32), pixel_recv.at[0, q, i])
-            piece = pixel_rows(owner, 32 * q + 16 * i, 16)
+            arrive(pixel_rows(owner, 0, 64), pixel_recv.at[0, q, i])
+            piece = pixel_rows(owner, 32 * i, 32)
             send(piece, piece, pixel_send.at[1, q, i], pixel_recv.at[1, q, i], z_peer[k])
-            whole = pixel_rows(owner, 32 * q, 32)
+            whole = pixel_rows(owner, 0, 64)
             send(whole, whole, pixel_send.at[3, q, i], pixel_recv.at[3, q, i], twin)
 
     def pixels_far(q):
         owner = turn(z, 2) * 2 + core
         for i in range(2):
-            piece = pixel_rows(owner, 32 * q + 16 * i, 16)
+            piece = pixel_rows(owner, 32 * i, 32)
             arrive(piece, pixel_recv.at[1, q, i])
-        whole = pixel_rows(owner, 32 * q, 32)
+        whole = pixel_rows(owner, 0, 64)
         send(whole, whole, pixel_send.at[4, q, 0], pixel_recv.at[4, q, 0], twin)
 
     def pixels_end():
         arrive(pixel_rows(z * 2 + 1 - core, 0, 64), pixel_recv.at[2, 0, 0])
-        for q in range(2):
+        for q in range(1):
             for i, k in enumerate((1, 3)):
-                arrive(pixel_rows(turn(z, 4 - k) * 2 + 1 - core, 32 * q, 32), pixel_recv.at[3, q, i])
-            arrive(pixel_rows(turn(z, 2) * 2 + 1 - core, 32 * q, 32), pixel_recv.at[4, q, 0])
+                arrive(pixel_rows(turn(z, 4 - k) * 2 + 1 - core, 0, 64), pixel_recv.at[3, q, i])
+            arrive(pixel_rows(turn(z, 2) * 2 + 1 - core, 0, 64), pixel_recv.at[4, q, 0])
 
     def sector_columns(owner_row):
         return sector_ref.at[:, pl.ds(pl.multiple_of(owner_row * 128, 128), 128)]
@@ -243,6 +250,8 @@
     for k in range(1, 16):
         source = row * 16 + turn(y, (16 - k) // 4 if k % 4 == 0 else 4 - k // 4) * 4 + turn(x, 4 - k % 4)
         arrive(all_ref.at[pl.ds(source, 1)], block_recv.at[k - 1])
+
+    own_rows.wait()
 
     def block_part(zs, which):
         return all_ref.at[pl.ds(zs * 32 + which * 16, 16), :, pl.ds(0, 128 * (zs + 1))]
@@ -309,11 +318,11 @@
                     device_id=x_peer[k], device_id_type=MESH,
                 ).start()
 
+    local.append(sectors_start())
     block_relay(0)
+    pass_x_other(0)
     block_ready(0)
     load_rows(0)
-    local.append(sectors_start())
-    pass_x_other(0)
 
     def rest_of_block():
         for zs in (1, 2, 3):
@@ -326,40 +335,62 @@
         (1, 0): [lambda: pass_on(0)],
         (1, 3): [lambda: pass_x_other(2)],
         (1, 8): [lambda: pass_on(1)],
-        (1, 10): [lambda: pixels_on(0)],
-        (1, 13): [lambda: pixels_on(1)],
+        (1, 14): [lambda: pixels_on(0)],
         (1, 15): [lambda: pass_x_other(3)],
         (2, 4): [lambda: pass_on(2), lambda: far_x(0)],
         (2, 10): [lambda: far_x(1), lambda: twin_rows(0, 2)],
         (2, 15): [lambda: pass_on(3)],
-        (3, 0): [lambda: pixels_far(0)],
-        (3, 4): [lambda: pixels_far(1)],
+        (3, 4): [lambda: pixels_far(0)],
         (3, 8): [lambda: far_x(2)],
         (3, 12): [lambda: far_x(3), lambda: twin_rows(1, 2)],
     }
 
     n = inverse_ref.shape[0]
     inverse_ref[...] = jnp.zeros_like(inverse_ref)
+    later = []
     for b in range(n // 128):
         s, e = b * 128, b * 128 + 128
+        jobs, later = later, []
 
         def store(g, value):
             inverse_ref[s + 8 * g : s + 8 * g + 8, s:e] = value
 
         def after(g):
+            if g == 0:
+                for job in jobs:
+                    job()
             for action in plan.get((b, g), ()):
                 action()
 
         invert_tile(m_ref[s:e, s:e], store, after)
-        inverse = inverse_ref[s:e, s:e]
+
+        if e < n:
+            below_ref[e:] = dot_nt(m_ref[e:, s:e], inverse_ref[s:e, s:e])
+            near = below_ref[e : e + 128]
+            m_ref[e : e + 128, e : e + 128] -= dot_nt(near, near)
+
+        def finish_row(s=s, e=e):
+            inverse_ref[s:e, :s] = dot_nn(inverse_ref[s:e, s:e], m_ref[s:e, :s])
+
+        def update_rest(s=s, e=e):
+            m_ref[e + 128 :, e:] -= dot_nt(below_ref[e + 128 :], below_ref[e:])
+
+        def update_left(s=s, e=e):
+            m_ref[e:, :s] -= dot_nn(below_ref[e:], inverse_ref[s:e, :s])
+
+        def update_here(s=s, e=e):
+            m_ref[e:, s:e] = -dot_nn(below_ref[e:], inverse_ref[s:e, s:e])
+
         if b:
-            inverse_ref[s:e, :s] = dot_nn(inverse, m_ref[s:e, :s])
+            later.append(finish_row)
         if e < n:
-            below = dot_nt(m_ref[e:, s:e], inverse)
-            m_ref[e:, e:] -= dot_nt(below, below)
+            if e + 128 < n:
+                later.append(update_rest)
             if b:
-                m_ref[e:, :s] -= dot_nn(below, inverse_ref[s:e, :s])
-            m_ref[e:, s:e] = -dot_nn(below, inverse)
+                later.append(update_left)
+            later.append(update_here)
+    for job in later:
+        job()
 
     pixels_end()
     sectors_end()
@@ -399,16 +430,17 @@
             jax.ShapeDtypeStruct((512, 2048), jnp.float32),
             jax.ShapeDtypeStruct((512, 128), jnp.float32),
         ),
-        in_specs=[pl.BlockSpec(memory_space=pltpu.VMEM), anywhere, anywhere, anywhere],
+        in_specs=[anywhere] * 4,
         out_specs=(pl.BlockSpec(memory_space=pltpu.VMEM), anywhere, anywhere, anywhere),
         scratch_shapes=[
             pltpu.VMEM((128, 4, 512), jnp.float32),
             pltpu.VMEM((512, 512), jnp.float32),
+            pltpu.VMEM((512, 128), jnp.float32),
             dma((22,)), dma((23,)),
             dma((4, CHUNKS, 3)), dma((7, CHUNKS)),
             dma((5, 2, 2)), dma((5, 2, 2)),
             dma((7,)), dma((7,)),
-            dma((2,)),
+            dma((3,)),
         ],
         compiler_params=pltpu.CompilerParams(
             collective_id=0, has_side_effects=True, vmem_limit_bytes=16 << 20
@@ -417,7 +449,7 @@
             flops=40_000_000_000, bytes_accessed=16 << 20, transcendentals=0
         ),
         name="panel",
-    )(own.reshape(1, 4, 512), cross, pixels, sectors)
+    )(own, cross, pixels, sectors)
 
 
 def high_low(value):
@@ -457,14 +489,29 @@
         lane = lax.broadcasted_iota(jnp.int32, own.shape, 1)
         line = lax.broadcasted_iota(jnp.int32, own.shape, 0) + device * 4
         factor_out[...] = jnp.where(lane <= line, own, 0.0)
-        columns = mxu(left_cat(cross_ref[...]), by_column, 1, 1)
+        lower = right_cat(inverse[:256, :256], 1)
+        last = right_cat(inverse[256:, 256:], 0)
+
+        def times_upper(value):
+            high, low = high_low(value)
+            near = jnp.concatenate([high[:, :256], high[:, :256], low[:, :256]], axis=1)
+            full = jnp.concatenate([high, high, low], axis=1)
+            return jnp.concatenate(
+                [mxu(near, lower, 1, 1), mxu(full, by_column[256:], 1, 1)], axis=1
+            )
+
+        columns = times_upper(cross_ref[...])
         columns_out[...] = columns
         columns_cat[...] = right_cat(columns, 1)
         for i in range(4):
             part = slice(256 * i, 256 * i + 256)
-            panel_rows = left_cat(mxu(left_cat(rows_ref[i]), by_column, 1, 1))
+            high, low = high_low(times_upper(rows_ref[i]))
+            panel_rows = jnp.concatenate([high, high, low], axis=1)
             rows_cat[part] = panel_rows
-            coupling_cat[part] = left_cat(mxu(panel_rows, by_row, 1, 0))
+            far = jnp.concatenate([high[:, 256:], high[:, 256:], low[:, 256:]], axis=1)
+            coupling_cat[part] = left_cat(jnp.concatenate(
+                [mxu(panel_rows, by_row[:, :256], 1, 0), mxu(far, last, 1, 0)], axis=1
+            ))
         solved = mxu(left_cat(inverse), right_cat(sectors_ref[...], 0), 1, 0)
         solved_cat = right_cat(solved, 0)
         sectors_out[...] = trail_sectors_ref[...] - mxu(left_cat(columns), solved_cat, 1, 0)
@@ -523,7 +570,7 @@
 ):
     in_hbm = lambda v: pltpu.with_memory_space_constraint(v, pltpu.HBM)
     inverse, rows, pixels, sectors = panel(
-        panel_block, in_hbm(panel_cross), in_hbm(panel_pixels), in_hbm(panel_sectors)
+        in_hbm(panel_block.reshape(1, 4, 512)), in_hbm(panel_cross), in_hbm(panel_pixels), in_hbm(panel_sectors)
     )
     return products(
         panel_block, panel_cross, rows, inverse, sectors, trail_sectors, trail_block, pixels, trail_pixels

time: 66 us -> 64.8 us (0.982)
  local copies, waits for them, and re-layouts: 0.71 us -> 0.02 us
    pallas_call x1, Pallas kernels: 18.7 us -> 17.7 us  [products(): pl.pallas_call(product_kernel, grid=(steps,), out_shape=(f32(*own.shape),...]
    unnamed x12 -> x10, local copies, waits for them, and re-layouts: 0.71 us -> 0.02 us
where the time goes in v2:
time: 64.8 us; the launch traced here: 64.6 us
  Pallas kernels  63.9 us (99%)
  between operations  0.72 us (1%)
    pallas_call x1, Pallas kernels, panel(): pl.pallas_call(panel_kernel, out_shape=(jax.ShapeDtypeStruct((512, 512),...  46.2 us
    pallas_call x1, Pallas kernels, products(): pl.pallas_call(product_kernel, grid=(steps,), out_shape=(f32(*own.shape),...  17.7 us

profile of v2, /device:TPU:1, one launch (start us, length us, event | category | flops | bytes accessed | tf_op | source)
XLA Modules:
  0.0 64.6 jit_solution(9035165832673158535)
XLA Ops:
  0.6 0.0 copy-start
  0.6 0.0 copy-start.1
  0.7 0.0 copy-start.2
  0.7 0.0 copy-start.3
  0.7 0.0 copy-start.4
  0.7 46.2 %panel.1 = (f32[512,512]{1,0:T(8,128)S(1)}, f32[6,256,512]{2,1,0:T(8,128)S(1)}, f32[512,2048]{1,0:T(8,128)S(1)}, f32[512,128]{1,0:T(8,128)S(1)}) custom-call(f32[1,4,512]{2,1,0:T(4,128)} %bitcast.1, f32[512,512]{1,0:T(8,128)} %cross_ref.3, f32[64,2048]{1,0:T(8,128)} %pixel_ref.1, f32[64,1024]{1,0:T(8,128)} %sector_ref.1), custom_call_target="tpu_custom_call" | custom-call | flops 40000000000 | bytes 16777216 | tf_op jit(solution)/shard_map/panel/pallas_call | solution.py:425
  46.9 0.0 copy-done
  46.9 0.0 copy-done.1
  46.9 0.0 copy-done.2
  46.9 0.0 copy-done.3
  46.9 0.0 copy-done.4
  46.9 17.7 %products.1 = (f32[4,512]{1,0:T(4,128)}, f32[512,512]{1,0:T(8,128)}, f32[1024,512]{1,0:T(8,128)}, f32[1024,2048]{1,0:T(8,128)}, f32[512,128]{1,0:T(8,128)}, /*index=5*/f32[2048,128]{1,0:T(8,128)}) custom-call(f32[4,512]{1,0:T(4,128)S(1)} %copy-done.4, f32[512,512]{1,0:T(8,128)S(1)} %copy-done.2, f32[6,256,512]{2,1,0:T(8,128)S(1)} %get-tuple-element.10.rows_ref, ...), custom_call_target="tpu_custom_call" | custom-call | flops 13500000256 | bytes 33554432 | tf_op jit(solution)/shard_map/products/pallas_call | solution.py:541
Async XLA Ops:
  0.6 46.2 %copy-start = (f32[1024,2048]{1,0:T(8,128)S(1)}, f32[1024,2048]{1,0:T(8,128)}, u32[]{:S(2)}) copy-start(f32[1024,2048]{1,0:T(8,128)} %trail_pixels_ref.1) | copy-start | bytes 25165828
  0.6 46.2 %copy-start.1 = (f32[1024,512]{1,0:T(8,128)S(1)}, f32[1024,512]{1,0:T(8,128)}, u32[]{:S(2)}) copy-start(f32[1024,512]{1,0:T(8,128)} %trail_ref.1) | copy-start | bytes 6291460
  0.7 46.2 %copy-start.2 = (f32[512,512]{1,0:T(8,128)S(1)}, f32[512,512]{1,0:T(8,128)}, u32[]{:S(2)}) copy-start(f32[512,512]{1,0:T(8,128)} %cross_ref.3) | copy-start | bytes 3145732
  0.7 46.2 %copy-start.3 = (f32[512,128]{1,0:T(8,128)S(1)}, f32[512,128]{1,0:T(8,128)}, u32[]{:S(2)}) copy-start(f32[512,128]{1,0:T(8,128)} %trail_sectors_ref.1) | copy-start | bytes 786436
  0.7 46.2 %copy-start.4 = (f32[4,512]{1,0:T(4,128)S(1)}, f32[4,512]{1,0:T(4,128)}, u32[]{:S(2)}) copy-start(f32[4,512]{1,0:T(4,128)} %own_ref.1) | copy-start | bytes 24580

commit v3 on v2

--- a/solution.py
+++ b/solution.py
@@ -319,6 +319,7 @@
                 ).start()
 
     local.append(sectors_start())
+    inverse_ref[...] = jnp.zeros_like(inverse_ref)
     block_relay(0)
     pass_x_other(0)
     block_ready(0)
@@ -346,7 +347,6 @@
     }
 
     n = inverse_ref.shape[0]
-    inverse_ref[...] = jnp.zeros_like(inverse_ref)
     later = []
     for b in range(n // 128):
         s, e = b * 128, b * 128 + 128
@@ -503,9 +503,9 @@
         columns = times_upper(cross_ref[...])
         columns_out[...] = columns
         columns_cat[...] = right_cat(columns, 1)
-        for i in range(4):
-            part = slice(256 * i, 256 * i + 256)
-            high, low = high_low(times_upper(rows_ref[i]))
+        for i in range(2):
+            part = slice(512 * i, 512 * i + 512)
+            high, low = high_low(times_upper(rows_ref[2 * i : 2 * i + 2].reshape(512, 512)))
             panel_rows = jnp.concatenate([high, high, low], axis=1)
             rows_cat[part] = panel_rows
             far = jnp.concatenate([high[:, 256:], high[:, 256:], low[:, 256:]], axis=1)

time: 64.8 us -> 64.7 us (level)
  no operation moved by 1% of the time
where the time goes in v3:
time: 64.7 us; the launch traced here: 64.6 us
  Pallas kernels  63.8 us (99%)
  between operations  0.72 us (1%)
    pallas_call x1, Pallas kernels, panel(): pl.pallas_call(panel_kernel, out_shape=(jax.ShapeDtypeStruct((512, 512),...  46.2 us
    pallas_call x1, Pallas kernels, products(): pl.pallas_call(product_kernel, grid=(steps,), out_shape=(f32(*own.shape),...  17.7 us

profile of v3, /device:TPU:1, one launch (start us, length us, event | category | flops | bytes accessed | tf_op | source)
XLA Modules:
  0.0 64.6 jit_solution(11398083579059287876)
XLA Ops:
  0.6 0.0 copy-start
  0.6 0.0 copy-start.1
  0.7 0.0 copy-start.2
  0.7 0.0 copy-start.3
  0.7 0.0 copy-start.4
  0.7 46.2 %panel.1 = (f32[512,512]{1,0:T(8,128)S(1)}, f32[6,256,512]{2,1,0:T(8,128)S(1)}, f32[512,2048]{1,0:T(8,128)S(1)}, f32[512,128]{1,0:T(8,128)S(1)}) custom-call(f32[1,4,512]{2,1,0:T(4,128)} %bitcast.1, f32[512,512]{1,0:T(8,128)} %cross_ref.3, f32[64,2048]{1,0:T(8,128)} %pixel_ref.1, f32[64,1024]{1,0:T(8,128)} %sector_ref.1), custom_call_target="tpu_custom_call" | custom-call | flops 40000000000 | bytes 16777216 | tf_op jit(solution)/shard_map/panel/pallas_call | solution.py:425
  46.9 0.0 copy-done
  46.9 0.0 copy-done.1
  46.9 0.0 copy-done.2
  46.9 0.0 copy-done.3
  46.9 0.0 copy-done.4
  46.9 17.7 %products.1 = (f32[4,512]{1,0:T(4,128)}, f32[512,512]{1,0:T(8,128)}, f32[1024,512]{1,0:T(8,128)}, f32[1024,2048]{1,0:T(8,128)}, f32[512,128]{1,0:T(8,128)}, /*index=5*/f32[2048,128]{1,0:T(8,128)}) custom-call(f32[4,512]{1,0:T(4,128)S(1)} %copy-done.4, f32[512,512]{1,0:T(8,128)S(1)} %copy-done.2, f32[6,256,512]{2,1,0:T(8,128)S(1)} %get-tuple-element.10.rows_ref, ...), custom_call_target="tpu_custom_call" | custom-call | flops 13500000256 | bytes 33554432 | tf_op jit(solution)/shard_map/products/pallas_call | solution.py:541
Async XLA Ops:
  0.6 46.2 %copy-start = (f32[1024,2048]{1,0:T(8,128)S(1)}, f32[1024,2048]{1,0:T(8,128)}, u32[]{:S(2)}) copy-start(f32[1024,2048]{1,0:T(8,128)} %trail_pixels_ref.1) | copy-start | bytes 25165828
  0.6 46.2 %copy-start.1 = (f32[1024,512]{1,0:T(8,128)S(1)}, f32[1024,512]{1,0:T(8,128)}, u32[]{:S(2)}) copy-start(f32[1024,512]{1,0:T(8,128)} %trail_ref.1) | copy-start | bytes 6291460
  0.7 46.2 %copy-start.2 = (f32[512,512]{1,0:T(8,128)S(1)}, f32[512,512]{1,0:T(8,128)}, u32[]{:S(2)}) copy-start(f32[512,512]{1,0:T(8,128)} %cross_ref.3) | copy-start | bytes 3145732
  0.7 46.2 %copy-start.3 = (f32[512,128]{1,0:T(8,128)S(1)}, f32[512,128]{1,0:T(8,128)}, u32[]{:S(2)}) copy-start(f32[512,128]{1,0:T(8,128)} %trail_sectors_ref.1) | copy-start | bytes 786436
  0.7 46.2 %copy-start.4 = (f32[4,512]{1,0:T(4,128)S(1)}, f32[4,512]{1,0:T(4,128)}, u32[]{:S(2)}) copy-start(f32[4,512]{1,0:T(4,128)} %own_ref.1) | copy-start | bytes 24580
